TPU v7x, 32 devices: a whole 2x2x4 slice. The times are simulated.
32 devices in a mesh: seq: 8 (over z, x), dp: 4 (over y, core).
Axes of the slice: x: 2, y: 2, z: 4, core: 2. Of those that a mesh axis runs over, the one named last changes fastest.
Arguments:
- features: bfloat16 [4, 2048, 2048], P('dp', 'seq'), may hold values from -6 to 6
- key_proj: bfloat16 [4, 2048, 128], P('dp', 'seq'), may hold values from -6 to 6
- query_proj: bfloat16 [4, 2048, 128], P('dp', 'seq'), may hold values from -6 to 6
- log_decay: float32 [4, 32, 2048], P('dp', None, 'seq'), may hold values from -0.002 to 0
- doc_start: int32 [4, 2048], P('dp', 'seq'), may hold values from 0 to 1, as said below
- loss_weight: float32 [4, 2048], P('dp', 'seq'), may hold values from 0.25 to 6
- target: bfloat16 [4, 2048, 2048], P('dp', 'seq'), may hold values from -6 to 6
Outputs:
- outputs: bfloat16 [4, 2048, 2048], P('dp', 'seq')
- grad_features: bfloat16 [4, 2048, 2048], P('dp', 'seq')
- grad_keys: bfloat16 [4, 2048, 128], P('dp', 'seq')
- grad_queries: bfloat16 [4, 2048, 128], P('dp', 'seq')
- grad_decay: float32 [4, 32, 2048], P('dp', None, 'seq')
Inputs may be any that keep to these rules, and one draw needn't show every extreme that they name: `doc_start`: position 0 of every row begins a document; a document runs from its 1 to the next 1 or the row's end and holds at most 1024 tokens; every row holds one of exactly 1024.
All inputs are finite; a program needn't handle non-finite values.
Results may differ from a plain program's by a relative error of at most 0.0085.
Values sent between devices are 32-bit elements; how exact they have to be, the bound alone decides.
A program may use at most 64 MiB of HBM per device.

v0:
```python
import math

import jax
import jax.numpy as jnp
from jax import lax
from jax.sharding import PartitionSpec as P

BLOCK = 256
DOC_SHARDS = 4


exact_mode = lax.Precision.HIGHEST


def from_behind(block, axis, distance):
    devices = range(lax.axis_size(axis))
    route = [(i - distance, i) for i in devices if i - distance in devices]
    return lax.ppermute(block, axis, route)


def block_tail(values, key_rows, running, segment):
    last_segment = segment[-1]
    tail_weight = jnp.where(
        segment[None, :] == last_segment, jnp.exp(running[:, -1:] - running), 0.0
    )
    fresh = jnp.einsum(
        "sn,shp->hpn", key_rows, values * tail_weight.T[:, :, None], precision=exact_mode
    )
    keep_gain = jnp.exp(running[:, -1]) * (last_segment == 0).astype(jnp.float32)
    return (fresh, keep_gain)


def unpack(feature, key_in, decay_log, starts, key_scale):
    heads = decay_log.shape[0]
    length = feature.shape[0]
    values = feature.astype(jnp.float32).reshape(length, heads, feature.shape[1] // heads)
    key_rows = key_in.astype(jnp.float32) * key_scale
    running = jnp.cumsum(decay_log, axis=1)
    segment = jnp.cumsum(starts)
    return (values, key_rows, running, segment)


def block_step(carry_state, block_piece, key_scale):
    feature, key_in, query_in, decay_log, starts = block_piece
    values, key_rows, running, segment = unpack(feature, key_in, decay_log, starts, key_scale)
    query_rows = query_in.astype(jnp.float32)
    length = values.shape[0]
    position = jnp.arange(length)
    linked = (position[:, None] >= position[None, :]) & (segment[:, None] == segment[None, :])
    scores = jnp.dot(query_in, key_in.T, preferred_element_type=jnp.float32) * key_scale
    mixing = jnp.where(linked, scores, 0.0).astype(jnp.bfloat16)
    mixing = lax.optimization_barrier(mixing)
    lifted = (values * jnp.exp(-running).T[:, :, None]).astype(jnp.bfloat16).reshape(length, -1)
    lifted = lax.optimization_barrier(lifted)
    rise = jnp.exp(running).T
    inner_part = (
        jnp.dot(mixing, lifted, preferred_element_type=jnp.float32).reshape(values.shape)
        * rise[:, :, None]
    )
    opened = (segment == 0).astype(jnp.float32)
    entry_gain = rise * opened[:, None]
    carried = (
        jnp.einsum("tn,hpn->thp", query_rows, carry_state, precision=exact_mode)
        * entry_gain[:, :, None]
    )
    fresh, keep_gain = block_tail(values, key_rows, running, segment)
    new_state = keep_gain[:, None, None] * carry_state + fresh
    return (new_state, (inner_part + carried).reshape(length, -1))


def split_blocks(feature, key_in, query_in, decay_log, starts):
    blocks = feature.shape[0] // BLOCK
    heads = decay_log.shape[0]
    return (
        feature.reshape(blocks, BLOCK, feature.shape[1]),
        key_in.reshape(blocks, BLOCK, key_in.shape[1]),
        query_in.reshape(blocks, BLOCK, query_in.shape[1]),
        decay_log.reshape(heads, blocks, BLOCK).transpose(1, 0, 2),
        starts.reshape(blocks, BLOCK),
    )


def process(feature, key_in, query_in, decay_log, starts, carry_state):
    key_scale = 1.0 / math.sqrt(key_in.shape[1] * BLOCK)
    pieces = split_blocks(feature, key_in, query_in, decay_log, starts)

    def process_advance(current, block_piece):
        return block_step(current, block_piece, key_scale)

    final_state, results = lax.scan(process_advance, carry_state, pieces)
    return (results.reshape(feature.shape[0], feature.shape[1]), final_state)


def end_state(feature, key_in, query_in, decay_log, starts, carry_state):
    key_scale = 1.0 / math.sqrt(key_in.shape[1] * BLOCK)
    pieces = split_blocks(feature, key_in, query_in, decay_log, starts)

    def end_advance(current, block_piece):
        values, key_rows, running, segment = unpack(
            block_piece[0], block_piece[1], block_piece[3], block_piece[4], key_scale
        )
        fresh, keep_gain = block_tail(values, key_rows, running, segment)
        return (keep_gain[:, None, None] * current + fresh, None)

    final_state, unused = lax.scan(end_advance, carry_state, pieces)
    return final_state


def combine(earlier, latter):
    return (earlier[0] * latter[0], latter[1] + latter[0][:, None, None] * earlier[1])


def doubling_offsets():
    offsets = [1]
    covered = 1
    while covered < DOC_SHARDS:
        offsets.append(covered)
        covered = covered * 2
    return offsets


def body(features, key_proj, query_proj, log_decay, doc_start, loss_weight, target):
    feature = features[0]
    key_in = key_proj[0]
    query_in = query_proj[0]
    decay_log = log_decay[0]
    starts = doc_start[0]
    weight = loss_weight[0]
    target_row = target[0]
    heads = decay_log.shape[0]
    head_size = feature.shape[1] // heads
    length = feature.shape[0]
    weight_sum = lax.psum(jnp.sum(weight), ("seq", "dp"))
    token_count = loss_weight.size * lax.axis_size("seq") * lax.axis_size("dp")
    mean_weight = weight_sum / token_count
    empty_state = jnp.zeros((heads, head_size, key_in.shape[1]), jnp.float32)
    fresh = end_state(feature, key_in, query_in, decay_log, starts, empty_state)
    carry_gain = jnp.exp(jnp.sum(decay_log, axis=1)) * (jnp.sum(starts) == 0).astype(jnp.float32)
    identity = (jnp.ones_like(carry_gain), jnp.zeros_like(fresh))
    source = (carry_gain, fresh)
    prior_pair = identity
    for step_by in doubling_offsets():
        arrived = from_behind((source[0], source[1]), "seq", step_by)
        prior_pair = combine(arrived, prior_pair)
        source = prior_pair
    prior_state = prior_pair[1]

    def forward(first, second, third, fourth):
        return process(first, second, third, fourth, starts, prior_state)

    primal, pullback = jax.vjp(forward, feature, key_in, query_in, decay_log)
    output = primal[0]
    grad_out = (weight / mean_weight)[:, None] * (output - target_row.astype(jnp.float32))
    opened = (jnp.cumsum(starts) == 0).astype(jnp.float32)
    factor = (jnp.exp(jnp.cumsum(decay_log, axis=1)) * opened[None, :]).T
    through = jnp.einsum(
        "tn,thp->hpn",
        query_in.astype(jnp.float32),
        grad_out.reshape(length, heads, head_size) * factor[:, :, None],
        precision=exact_mode,
    )
    source = (carry_gain, through)
    adjoint = identity
    for step_by in doubling_offsets():
        arrived = from_behind((source[0], source[1]), "seq", -step_by)
        adjoint = combine(arrived, adjoint)
        source = adjoint
    gradients = pullback((grad_out, adjoint[1]))
    return (
        output.astype(jnp.bfloat16)[None],
        gradients[0][None],
        gradients[1][None],
        gradients[2][None],
        gradients[3][None],
    )


def solution(mesh):
    placed = (
        P("dp", "seq", None),
        P("dp", "seq", None),
        P("dp", "seq", None),
        P("dp", None, "seq"),
        P("dp", "seq"),
        P("dp", "seq"),
        P("dp", "seq", None),
    )
    return jax.shard_map(
        body,
        mesh=mesh,
        in_specs=placed,
        out_specs=(
            P("dp", "seq", None),
            P("dp", "seq", None),
            P("dp", "seq", None),
            P("dp", "seq", None),
            P("dp", None, "seq"),
        ),
        check_vma=False,
    )
```

profile of v0, /device:TPU:0, one launch (start us, length us, event | category | flops | bytes accessed | tf_op | source)
XLA Modules:
  0.0 240.9 jit_solution(7249598371111277392)
XLA Ops:
  0.6 1.0 reduce-window.36
  2.0 0.6 slice.43
  3.2 0.7 broadcast_compare_fusion
  3.9 0.8 reshape.321
  4.7 0.6 reduce-window.38
  5.3 0.2 slice_reduce_fusion.1
  5.7 0.8 multiply_bitcast_fusion
  6.5 1.5 copy.72
  8.1 0.1 bitcast_multiply_fusion.2
  8.2 0.7 copy-done.12
  8.9 1.8 convolution_add_fusion
  10.7 4.9 %collective-permute-start = (f32[32,64,128]{2,1,0:T(8,128)S(1)}, f32[32,64,128]{2,1,0:T(8,128)S(1)}, u32[]{:S(2)}, u32[]{:S(2)}) collective-permute-start(f32[32,64,128]{2,1,0:T(8,128)S(1)} %convolution_add_fusion), channel_id=1, source_target_pairs={{0,4},{4,8},{8,12},{12,16},{16,20},{20,24},{24,28},{1,5},{5,9},{9,... | collective-permute-start | bytes 3145736 | tf_op jit(solution)/shard_map/ppermute | solution.py:18
  15.6 22.3 %collective-permute-done = f32[32,64,128]{2,1,0:T(8,128)S(1)} collective-permute-done((f32[32,64,128]{2,1,0:T(8,128)S(1)}, f32[32,64,128]{2,1,0:T(8,128)S(1)}, u32[]{:S(2)}, u32[]{:S(2)}) %collective-permute-start) | collective-permute-done | bytes 1048608 | tf_op jit(solution)/shard_map/ppermute | solution.py:18
  38.0 5.4 %collective-permute-start.2 = (f32[32,64,128]{2,1,0:T(8,128)S(1)}, f32[32,64,128]{2,1,0:T(8,128)}, u32[]{:S(2)}, u32[]{:S(2)}) collective-permute-start(f32[32,64,128]{2,1,0:T(8,128)S(1)} %collective-permute-done), channel_id=1, source_target_pairs={{0,4},{4,8},{8,12},{12,16},{16,20},{20,24},{24,28},{1,5},{5,9},{9,... | collective-permute-start | bytes 3145736 | tf_op jit(solution)/shard_map/ppermute | solution.py:18
  43.3 0.6 reduce_sum.113
  44.8 3.9 %collective-permute-start.1 = (f32[32]{0:T(128)S(1)}, f32[32]{0:T(128)}, u32[]{:S(2)}, u32[]{:S(2)}) collective-permute-start(f32[32]{0:T(128)S(1)} %exponential_multiply_fusion), channel_id=1, source_target_pairs={{0,4},{4,8},{8,12},{12,16},{16,20},{20,24},{24,28},{1,5},{5,9},{9,... | collective-permute-start | bytes 392 | tf_op jit(solution)/shard_map/ppermute | solution.py:18
  48.7 15.2 %collective-permute-done.1 = f32[32]{0:T(128)} collective-permute-done((f32[32]{0:T(128)S(1)}, f32[32]{0:T(128)}, u32[]{:S(2)}, u32[]{:S(2)}) %collective-permute-start.1) | collective-permute-done | bytes 160 | tf_op jit(solution)/shard_map/ppermute | solution.py:18
  63.9 1.4 multiply_add_fusion.3
  65.3 7.4 %collective-permute-start.4 = (f32[32,64,128]{2,1,0:T(8,128)S(1)}, f32[32,64,128]{2,1,0:T(8,128)}, u32[]{:S(2)}, u32[]{:S(2)}) collective-permute-start(f32[32,64,128]{2,1,0:T(8,128)S(1)} %multiply_add_fusion.3), channel_id=1, source_target_pairs={{0,8},{4,12},{8,16},{12,20},{16,24},{20,28},{1,9},{5,13},{9,17},{1... | collective-permute-start | bytes 3145736 | tf_op jit(solution)/shard_map/ppermute | solution.py:18
  72.7 0.6 reduce_sum.114
  73.3 41.3 %psum.7 = f32[]{:T(128)} all-reduce(f32[]{:T(128)} %reduce_sum.114), channel_id=1, replica_groups=mesh['seq'=8,'dp'=4] {'seq','dp'}, use_global_device_ids=true, to_apply=%region_7.8 | all-reduce | flops 1 | bytes 8 | tf_op jit(solution)/shard_map/psum | solution.py:133
  114.7 0.7 copy.83
  115.4 1.0 fusion.10
  116.5 1.6 copy.85
  118.0 1.0 copy.76
  119.0 1.6 copy.79
  120.6 0.2 fusion.2
  121.5 0.7 broadcast_divide_fusion
  122.2 1.8 fusion.81
  124.0 4.7 %collective-permute-start.3 = (f32[32]{0:T(128)}, f32[32]{0:T(128)}, u32[]{:S(2)}, u32[]{:S(2)}) collective-permute-start(f32[32]{0:T(128)} %collective-permute-done.1), channel_id=1, source_target_pairs={{0,4},{4,8},{8,12},{12,16},{16,20},{20,24},{24,28},{1,5},{5,9},{9,... | collective-permute-start | bytes 392 | tf_op jit(solution)/shard_map/ppermute | solution.py:18
  128.7 2.5 %copy.84 = f32[1,256,2048]{1,2,0:T(8,128)} copy(bf16[1,256,2048]{2,1,0:T(8,128)(2,1)} %param.13) | data formatting | bytes 3145728 | tf_op jit(solution)/shard_map/convert_element_type | solution.py:153
  131.2 0.8 mul.347
  132.0 1.4 multiply_add_fusion.2
  133.5 5.2 %fusion.1 = (f32[256,32]{0,1:T(8,128)}, f32[256,32]{0,1:T(8,128)}, f32[256,32,64]{0,2,1:T(8,128)S(1)}, bf16[256,32,64]{0,2,1:T(8,128)(2,1)}) fusion(f32[256,2048]{0,1:T(8,128)S(1)} %copy-done.2, f32[256,32,64]{0,2,1:T(8,128)} %bitcast.155, f32[256,32]{0,1:T(8,128)S(1)} %copy-done.9, f32[256,32]{0,1:T(8,128)S(1)} %copy-done.11, f32[256]{0:T(256)S(1)} %bitcast.162, ...), kind=kOutput, calls=%fused_computation.4 | convolution fusion | flops 811581440 | bytes 10683392 | tf_op jit(solution)/shard_map/jvp()/while/body/eval_jaxpr/tn,hpn->thp/dot_general | solution.py:63
  138.7 1.1 fusion.7
  139.8 1.3 collective-permute-start.5
  141.1 24.6 %collective-permute-done.5 = f32[32,64,128]{2,1,0:T(8,128)S(1)} collective-permute-done((f32[32,64,128]{2,1,0:T(8,128)S(1)}, f32[32,64,128]{2,1,0:T(8,128)S(1)}, u32[]{:S(2)}, u32[]{:S(2)}) %collective-permute-start.5) | collective-permute-done | bytes 1048608 | tf_op jit(solution)/shard_map/ppermute | solution.py:18
  165.8 1.3 collective-permute-start.7
  167.1 1.3 collective-permute-start.6
  168.4 22.5 %collective-permute-done.6 = f32[32]{0:T(128)S(1)} collective-permute-done((f32[32]{0:T(128)S(1)}, f32[32]{0:T(128)S(1)}, u32[]{:S(2)}, u32[]{:S(2)}) %collective-permute-start.6) | collective-permute-done | bytes 160 | tf_op jit(solution)/shard_map/ppermute | solution.py:18
  190.8 1.3 collective-permute-start.8
  192.1 4.1 %collective-permute-done.8 = f32[32]{0:T(128)S(1)} collective-permute-done((f32[32]{0:T(128)S(1)}, f32[32]{0:T(128)S(1)}, u32[]{:S(2)}, u32[]{:S(2)}) %collective-permute-start.8) | collective-permute-done | bytes 160 | tf_op jit(solution)/shard_map/ppermute | solution.py:18
  196.2 0.3 broadcast_multiply_fusion
  196.5 1.2 multiply_add_fusion.1
  197.7 1.3 collective-permute-start.9
  199.0 1.1 fusion.83
  200.1 1.5 copy.88
  201.6 1.5 copy.89
  203.2 2.7 %fusion.82 = bf16[256,2048]{1,0:T(8,128)(2,1)} fusion(bf16[256,256]{1,0:T(8,128)(2,1)S(1)} %fusion.10, bf16[256,2048]{0,1:T(8,128)(2,1)} %bitcast.153), kind=kOutput, calls=%fused_computation.107 | convolution fusion | flops 268435456 | bytes 2228224 | tf_op jit(solution)/shard_map/transpose(jvp())/while/body/eval_jaxpr/dot_general | solution.py:57
  205.9 2.6 %copy.86 = f32[256,2048]{0,1:T(8,128)} copy(bf16[256,2048]{1,0:T(8,128)(2,1)} %fusion.82) | data formatting | bytes 3145728 | tf_op jit(solution)/shard_map/transpose(jvp())/while/body/eval_jaxpr/convert_element_type | solution.py:53
  208.5 2.3 copy.93
  210.8 1.2 convolution_convert_fusion.2
  212.0 1.8 convolution_convert_fusion.3
  213.9 5.3 %fusion.35 = bf16[1,256,128]{2,1,0:T(8,128)(2,1)} fusion(bf16[256,128]{1,0:T(8,128)(2,1)S(1)} %convolution_convert_fusion.2, f32[32,64,128]{2,1,0:T(8,128)} %copy-done.3, f32[256,32,64]{0,2,1:T(8,128)S(1)} %get-tuple-element.187, f32[256,32]{0,1:T(8,128)S(1)} %copy-done.10), kind=kOutput, calls=%fused_computation.34 | convolution fusion | flops 805896192 | bytes 3309568 | tf_op jit(solution)/shard_map/transpose(jvp())/while/body/eval_jaxpr/tn,hpn->thp/dot_general | solution.py:63
  219.2 1.7 collective-permute-done.9
  220.9 2.1 multiply_reduce_fusion.3
  223.0 4.4 %multiply_reduce_fusion.2 = (f32[256,32]{0,1:T(8,128)}, f32[256,32]{0,1:T(8,128)}, f32[256,32,64]{0,2,1:T(8,128)}, bf16[256,32,64]{0,2,1:T(8,128)(2,1)S(1)}) fusion(f32[256,2048]{0,1:T(8,128)S(1)} %copy-done.1, bf16[256,32,64]{0,2,1:T(8,128)(2,1)S(1)} %bitcast.151, f32[256,32,64]{0,2,1:T(8,128)S(1)} %bitcast.149, f32[256,32]{0,1:T(8,128)S(1)} %copy.76, ...), kind=kOutput, calls=%fused_computation.10 | convolution fusion | flops 810074112 | bytes 9633792 | tf_op jit(solution)/shard_map/transpose(jvp())/while/body/eval_jaxpr/sn,shp->hpn/dot_general | solution.py:26
  227.4 0.9 copy.87
  228.4 0.9 copy.90
  229.3 1.0 fusion.46
  230.4 2.5 %reduce-window.40 = f32[32,2,128]{2,0,1:T(8,128)S(1)} reduce-window(f32[32,2,128]{2,0,1:T(8,128)S(1)} %copy.91, f32[]{:T(128)} %constant.163.clone.1), window={size=1x1x128 pad=0_0x0_0x0_127}, to_apply=%region_14.15 | reduce-window | flops 1040384 | bytes 65540 | tf_op jit(solution)/shard_map/reduce-window.8
  233.2 0.6 reduce_window_sum.90
  233.8 1.4 copy.94
  235.2 5.7 %fusion.29 = bf16[1,256,128]{2,1,0:T(8,128)(2,1)} fusion(bf16[256,128]{1,0:T(8,128)(2,1)S(1)} %copy-done.17, f32[32,64,128]{2,1,0:T(8,128)S(1)} %get-tuple-element.186, f32[256,32,64]{0,2,1:T(8,128)} %get-tuple-element.188, f32[256,32]{0,1:T(8,128)S(1)} %copy.82), kind=kOutput, calls=%fused_computation.32 | convolution fusion | flops 805928960 | bytes 3309568 | tf_op jit(solution)/shard_map/transpose(jvp())/while/body/eval_jaxpr/sn,shp->hpn/dot_general | solution.py:26
  (75 shorter events, 1.4 us)
Async XLA Ops:
  0.6 114.8 %copy-start = (bf16[1,256,128]{2,1,0:T(8,128)(2,1)S(1)}, bf16[1,256,128]{2,1,0:T(8,128)(2,1)}, u32[]{:S(2)}) copy-start(bf16[1,256,128]{2,1,0:T(8,128)(2,1)} %param.9) | copy-start | bytes 196612
  2.0 113.5 %copy-start.18 = (s32[256]{0:T(256)}, s32[256]{0:T(256)S(1)}, u32[]{:S(2)}) copy-start(s32[256]{0:T(256)S(1)} %get-tuple-element.190) | copy-start | bytes 3076
  8.0 0.8 copy-start.12
  8.2 35.1 %copy-start.20 = (s32[1,256]{1,0:T(1,128)S(1)}, s32[1,256]{1,0:T(1,128)}, u32[]{:S(2)}) copy-start(s32[1,256]{1,0:T(1,128)} %param.11) | copy-start | bytes 3076
  8.2 35.8 %copy-start.16 = (f32[1,32,256]{2,1,0:T(8,128)S(1)}, f32[1,32,256]{2,1,0:T(8,128)}, u32[]{:S(2)}) copy-start(f32[1,32,256]{2,1,0:T(8,128)} %param.10) | copy-start | bytes 98308
  10.7 62.0 %copy-start.21 = (f32[1,256]{1,0:T(1,128)S(1)}, f32[1,256]{1,0:T(1,128)}, u32[]{:S(2)}) copy-start(f32[1,256]{1,0:T(1,128)} %param.12) | copy-start | bytes 3076
  10.7 27.2 %collective-permute-start = (f32[32,64,128]{2,1,0:T(8,128)S(1)}, f32[32,64,128]{2,1,0:T(8,128)S(1)}, u32[]{:S(2)}, u32[]{:S(2)}) collective-permute-start(f32[32,64,128]{2,1,0:T(8,128)S(1)} %convolution_add_fusion), channel_id=1, source_target_pairs={{0,4},{4,8},{8,12},{12,16},{16,20},{20,24},{24,28},{1,5},{5,9},{9,... | collective-permute-start | bytes 3145736 | tf_op jit(solution)/shard_map/ppermute | solution.py:18
  38.0 26.0 %collective-permute-start.2 = (f32[32,64,128]{2,1,0:T(8,128)S(1)}, f32[32,64,128]{2,1,0:T(8,128)}, u32[]{:S(2)}, u32[]{:S(2)}) collective-permute-start(f32[32,64,128]{2,1,0:T(8,128)S(1)} %collective-permute-done), channel_id=1, source_target_pairs={{0,4},{4,8},{8,12},{12,16},{16,20},{20,24},{24,28},{1,5},{5,9},{9,... | collective-permute-start | bytes 3145736 | tf_op jit(solution)/shard_map/ppermute | solution.py:18
  44.7 73.3 %copy-start.22 = (f32[32]{0:T(128)}, f32[32]{0:T(128)S(1)}, u32[]{:S(2)}) copy-start(f32[32]{0:T(128)S(1)} %exponential_multiply_fusion) | copy-start | bytes 388
  44.8 19.1 %collective-permute-start.1 = (f32[32]{0:T(128)S(1)}, f32[32]{0:T(128)}, u32[]{:S(2)}, u32[]{:S(2)}) collective-permute-start(f32[32]{0:T(128)S(1)} %exponential_multiply_fusion), channel_id=1, source_target_pairs={{0,4},{4,8},{8,12},{12,16},{16,20},{20,24},{24,28},{1,5},{5,9},{9,... | collective-permute-start | bytes 392 | tf_op jit(solution)/shard_map/ppermute | solution.py:18
  65.3 66.7 %collective-permute-start.4 = (f32[32,64,128]{2,1,0:T(8,128)S(1)}, f32[32,64,128]{2,1,0:T(8,128)}, u32[]{:S(2)}, u32[]{:S(2)}) collective-permute-start(f32[32,64,128]{2,1,0:T(8,128)S(1)} %multiply_add_fusion.3), channel_id=1, source_target_pairs={{0,8},{4,12},{8,16},{12,20},{16,24},{20,28},{1,9},{5,13},{9,17},{1... | collective-permute-start | bytes 3145736 | tf_op jit(solution)/shard_map/ppermute | solution.py:18
  120.8 10.4 %copy-start.5 = (bf16[256,2048]{0,1:T(8,128)(2,1)}, bf16[256,2048]{0,1:T(8,128)(2,1)S(1)}, u32[]{:S(2)}) copy-start(bf16[256,2048]{0,1:T(8,128)(2,1)S(1)} %fusion.2) | copy-start | bytes 3145732
  124.0 7.2 %collective-permute-start.3 = (f32[32]{0:T(128)}, f32[32]{0:T(128)}, u32[]{:S(2)}, u32[]{:S(2)}) collective-permute-start(f32[32]{0:T(128)} %collective-permute-done.1), channel_id=1, source_target_pairs={{0,4},{4,8},{8,12},{12,16},{16,20},{20,24},{24,28},{1,5},{5,9},{9,... | collective-permute-start | bytes 392 | tf_op jit(solution)/shard_map/ppermute | solution.py:18
  131.2 2.2 copy-start.2
  131.2 2.2 copy-start.9
  131.2 2.2 copy-start.11
  133.4 5.3 %copy-start.3 = (f32[32,64,128]{2,1,0:T(8,128)}, f32[32,64,128]{2,1,0:T(8,128)S(1)}, u32[]{:S(2)}) copy-start(f32[32,64,128]{2,1,0:T(8,128)S(1)} %multiply_add_fusion.2) | copy-start | bytes 3145732
  133.5 5.3 %copy-start.15 = (f32[256,32]{0,1:T(8,128)S(1)}, f32[256,32]{0,1:T(8,128)}, u32[]{:S(2)}) copy-start(f32[256,32]{0,1:T(8,128)} %copy.85) | copy-start | bytes 98308
  138.7 28.3 %copy-start.23 = (f32[32]{0:T(128)S(1)}, f32[32]{0:T(128)}, u32[]{:S(2)}) copy-start(f32[32]{0:T(128)} %copy-done.22) | copy-start | bytes 388
  139.8 25.9 %collective-permute-start.5 = (f32[32,64,128]{2,1,0:T(8,128)S(1)}, f32[32,64,128]{2,1,0:T(8,128)S(1)}, u32[]{:S(2)}, u32[]{:S(2)}) collective-permute-start(f32[32,64,128]{2,1,0:T(8,128)S(1)} %fusion.7), channel_id=1, source_target_pairs={{4,0},{8,4},{12,8},{16,12},{20,16},{24,20},{28,24},{5,1},{9,5},{13... | collective-permute-start | bytes 3145736 | tf_op jit(solution)/shard_map/ppermute | solution.py:18
  165.8 30.8 %collective-permute-start.7 = (f32[32,64,128]{2,1,0:T(8,128)S(1)}, f32[32,64,128]{2,1,0:T(8,128)S(1)}, u32[]{:S(2)}, u32[]{:S(2)}) collective-permute-start(f32[32,64,128]{2,1,0:T(8,128)S(1)} %collective-permute-done.5), channel_id=1, source_target_pairs={{4,0},{8,4},{12,8},{16,12},{20,16},{24,20},{28,24},{5,1},{9,5},{13... | collective-permute-start | bytes 3145736 | tf_op jit(solution)/shard_map/ppermute | solution.py:18
  167.1 23.8 %collective-permute-start.6 = (f32[32]{0:T(128)S(1)}, f32[32]{0:T(128)S(1)}, u32[]{:S(2)}, u32[]{:S(2)}) collective-permute-start(f32[32]{0:T(128)S(1)} %copy-done.23), channel_id=1, source_target_pairs={{4,0},{8,4},{12,8},{16,12},{20,16},{24,20},{28,24},{5,1},{9,5},{13... | collective-permute-start | bytes 392 | tf_op jit(solution)/shard_map/ppermute | solution.py:18
  190.8 5.4 %collective-permute-start.8 = (f32[32]{0:T(128)S(1)}, f32[32]{0:T(128)S(1)}, u32[]{:S(2)}, u32[]{:S(2)}) collective-permute-start(f32[32]{0:T(128)S(1)} %collective-permute-done.6), channel_id=1, source_target_pairs={{4,0},{8,4},{12,8},{16,12},{20,16},{24,20},{28,24},{5,1},{9,5},{13... | collective-permute-start | bytes 392 | tf_op jit(solution)/shard_map/ppermute | solution.py:18
  196.5 3.6 %copy-start.7 = (bf16[256,32,64]{0,2,1:T(8,128)(2,1)}, bf16[256,32,64]{0,2,1:T(8,128)(2,1)S(1)}, u32[]{:S(2)}) copy-start(bf16[256,32,64]{0,2,1:T(8,128)(2,1)S(1)} %broadcast_multiply_fusion) | copy-start | bytes 3145732
  196.5 2.5 %copy-start.6 = (bf16[256,2048]{0,1:T(8,128)(2,1)S(1)}, bf16[256,2048]{0,1:T(8,128)(2,1)}, u32[]{:S(2)}) copy-start(bf16[256,2048]{0,1:T(8,128)(2,1)} %copy-done.5) | copy-start | bytes 3145732
  197.7 23.2 %collective-permute-start.9 = (f32[32,64,128]{2,1,0:T(8,128)}, f32[32,64,128]{2,1,0:T(8,128)}, u32[]{:S(2)}, u32[]{:S(2)}) collective-permute-start(f32[32,64,128]{2,1,0:T(8,128)} %multiply_add_fusion.1), channel_id=1, source_target_pairs={{8,0},{12,4},{16,8},{20,12},{24,16},{28,20},{9,1},{13,5},{17,9},{2... | collective-permute-start | bytes 3145736 | tf_op jit(solution)/shard_map/ppermute | solution.py:18
  205.9 4.9 %copy-start.13 = (bf16[1,256,128]{2,1,0:T(8,128)(2,1)S(1)}, bf16[1,256,128]{2,1,0:T(8,128)(2,1)}, u32[]{:S(2)}) copy-start(bf16[1,256,128]{2,1,0:T(8,128)(2,1)} %param.8) | copy-start | bytes 196612
  205.9 4.9 %copy-start.19 = (s32[256]{0:T(256)S(1)}, s32[256]{0:T(256)}, u32[]{:S(2)}) copy-start(s32[256]{0:T(256)} %copy-done.18) | copy-start | bytes 3076
  208.5 5.4 %copy-start.10 = (f32[256,32]{0,1:T(8,128)S(1)}, f32[256,32]{0,1:T(8,128)}, u32[]{:S(2)}) copy-start(f32[256,32]{0,1:T(8,128)} %copy.83) | copy-start | bytes 98308
  210.8 10.1 %copy-start.4 = (f32[32,64,128]{2,1,0:T(8,128)S(1)}, f32[32,64,128]{2,1,0:T(8,128)}, u32[]{:S(2)}) copy-start(f32[32,64,128]{2,1,0:T(8,128)} %copy-done.3) | copy-start | bytes 3145732
  219.2 3.8 %copy-start.1 = (f32[256,2048]{0,1:T(8,128)S(1)}, f32[256,2048]{0,1:T(8,128)}, u32[]{:S(2)}) copy-start(f32[256,2048]{0,1:T(8,128)} %copy.86) | copy-start | bytes 6291460
  219.2 3.8 %copy-start.14 = (bf16[1,256,128]{2,1,0:T(8,128)(2,1)S(1)}, bf16[1,256,128]{2,1,0:T(8,128)(2,1)}, u32[]{:S(2)}) copy-start(bf16[1,256,128]{2,1,0:T(8,128)(2,1)} %param.8) | copy-start | bytes 196612
  223.0 6.3 %copy-start.8 = (f32[256,32]{1,0:T(8,128)S(1)}, f32[256,32]{1,0:T(8,128)}, u32[]{:S(2)}) copy-start(f32[256,32]{1,0:T(8,128)} %copy.88) | copy-start | bytes 98308
  227.4 7.8 %copy-start.17 = (bf16[256,128]{1,0:T(8,128)(2,1)S(1)}, bf16[256,128]{1,0:T(8,128)(2,1)}, u32[]{:S(2)}) copy-start(bf16[256,128]{1,0:T(8,128)(2,1)} %convolution_convert_fusion.3) | copy-start | bytes 196612
where the time goes:
time: 242 us; the launch traced here: 241 us
  waiting for transfers between devices  90.5 us (37%)
  blocking collectives  41.3 us (17%)
  matrix products  33.3 us (14%)
  starting transfers between devices  32.7 us (14%)
  local copies, waits for them, and re-layouts  23.4 us (10%)
  other arithmetic  16.6 us (7%)
  between operations  3.01 us (1%)
    ppermute x10, waiting for transfers between devices, from_behind(): return lax.ppermute(block, axis, route)  90.5 us
    psum x1, blocking collectives, body(): weight_sum = lax.psum(jnp.sum(weight), ('seq', 'dp'))  41.3 us
    ppermute x10, starting transfers between devices, from_behind(): return lax.ppermute(block, axis, route)  32.7 us
    dot_general x3, matrix products, block_tail(): jnp.einsum('sn,shp->hpn', key_rows, values * tail_weight.T[:, :, None], p...  11.9 us
    dot_general x2, matrix products, block_step(): jnp.einsum('tn,hpn->thp', query_rows, carry_state, precision=exact_mode)  10.5 us
    unnamed x51, local copies, waits for them, and re-layouts  5.94 us
    dot_general x3, matrix products, block_step(): jnp.dot(mixing, lifted, preferred_element_type=jnp.float32)  5.7 us
  transfers between devices with their start and end apart: 10, of which 6 were waited for; matrix products, arithmetic and copies ran while one was open for 14% of the time, Pallas kernels for 0%

commit v1 on v0

v1 whole, which is shorter than its diff:
```python
import functools
import math

import jax
import jax.numpy as jnp
from jax import lax
from jax.experimental import pallas as pl
from jax.experimental.pallas import tpu as pltpu
from jax.sharding import PartitionSpec as P

F32 = jnp.float32
BF16 = jnp.bfloat16
MESH = pl.DeviceIdType.MESH
CHUNK = 256
EXTRA = 8


def mm(a, b):
    return jnp.dot(a, b, preferred_element_type=F32)


def mm_nt(a, b):
    return lax.dot_general(a, b, (((1,), (1,)), ((), ())), preferred_element_type=F32)


def split(x):
    hi = x.astype(BF16)
    lo = (x - hi.astype(F32)).astype(BF16)
    return hi, lo


def kernel(
    n_seq, n_dp, heads,
    f_ref, k_ref, q_ref, ld_ref, ds_ref, w_ref, t_ref,
    out_ref, gf_ref, gk_ref, gq_ref, gd_ref,
    xf_send, xf_recv, zf_send, zf_recv, xb_send, xb_recv, zb_send, zb_recv,
    rise_s, inv_s, y_s, dl_s, lift_s, so_s,
    dmix_s, dmixt_s, dq_s, dk_s, rt_s, ex_s,
    wown, wseq, wrow, wdp,
    xfs, xfr, zfs, zfr, xbs, xbr, zbs, zbr, wss, wsr, wds, wdr,
):
    length, width = f_ref.shape
    state = k_ref.shape[1]
    head_size = width // heads
    chunks = width // CHUNK
    per_chunk = CHUNK // head_size
    sigma = 1.0 / math.sqrt(state * length)

    me = lax.axis_index("seq")
    row = lax.axis_index("dp")
    pair = me // 2
    pairs = n_seq // 2
    is_odd = me % 2
    odd = is_odd == 1
    partner = me + 1 - 2 * is_odd

    barrier = pltpu.get_barrier_semaphore()

    def greet_seq(d, _):
        pl.semaphore_signal(
            barrier, inc=1, device_id={"seq": (me + d) % n_seq}, device_id_type=MESH
        )
        return 0

    def greet_dp(d, _):
        pl.semaphore_signal(
            barrier, inc=1, device_id={"dp": (row + d) % n_dp}, device_id_type=MESH
        )
        return 0

    lax.fori_loop(1, n_seq, greet_seq, 0)
    lax.fori_loop(1, n_dp, greet_dp, 0)

    wown[...] = jnp.broadcast_to(jnp.sum(w_ref[...], axis=1, keepdims=True), wown.shape)

    starts = ds_ref[...].astype(F32)
    table = jnp.concatenate(
        [
            ld_ref[...],
            jnp.broadcast_to(starts, (8, length)),
            jnp.broadcast_to(w_ref[...], (8, length)),
            jnp.zeros((128 - heads - 16, length), F32),
        ],
        axis=0,
    )
    rows_i = lax.broadcasted_iota(jnp.int32, (length, length), 0)
    cols_i = lax.broadcasted_iota(jnp.int32, (length, length), 1)
    lower = (rows_i >= cols_i).astype(F32).astype(BF16)
    upper = (rows_i <= cols_i).astype(F32).astype(BF16)
    eye = (rows_i == cols_i).astype(F32).astype(BF16)
    eye_n = eye[:state, :state]
    table_hi, table_lo = split(table)
    cumulative = mm_nt(lower, table_hi) + mm_nt(lower, table_lo)
    turned = mm_nt(eye, table_hi) + mm_nt(eye, table_lo)
    seg_col = cumulative[:, heads:heads + 1]
    seg_row = mm(jnp.broadcast_to(starts, (8, length)).astype(BF16), upper)[0:1]
    last_seg = jnp.sum(starts, axis=1, keepdims=True)
    tail_row = (seg_row == last_seg).astype(F32)
    tail_col = (seg_col == last_seg).astype(F32)
    open_row = (seg_row == 0.0).astype(F32)
    open_col = (seg_col == 0.0).astype(F32)
    whole_block = (last_seg == 0.0).astype(F32)
    run_hi, run_lo = split(cumulative)

    keys = k_ref[...]
    queries = q_ref[...]
    keys_t = (mm_nt(eye_n, keys) * tail_row).astype(BF16)
    queries_t = (mm_nt(eye_n, queries) * open_row).astype(BF16)
    keys_tail = (keys.astype(F32) * tail_col).astype(BF16)
    queries_open = (queries.astype(F32) * open_col).astype(BF16)

    head_i = lax.broadcasted_iota(jnp.int32, (128, CHUNK), 0)
    lane_h = lax.broadcasted_iota(jnp.int32, (128, CHUNK), 1) // head_size

    def spread(c):
        return (head_i == lane_h + c * per_chunk).astype(F32).astype(BF16)

    def lanes(c):
        return pl.ds(pl.multiple_of(c * CHUNK, CHUNK), CHUNK)

    def to_partner(send, recv, ss, rs, c):
        return pltpu.make_async_remote_copy(
            src_ref=send.at[c], dst_ref=recv.at[c], send_sem=ss.at[c], recv_sem=rs.at[c],
            device_id={"seq": partner}, device_id_type=MESH,
        )

    def to_pair(send, recv, ss, rs, c, target):
        return pltpu.make_async_remote_copy(
            src_ref=send.at[c], dst_ref=recv.at[c], send_sem=ss.at[c], recv_sem=rs.at[c],
            device_id={"seq": target}, device_id_type=MESH,
        )

    def w_seq(d):
        return pltpu.make_async_remote_copy(
            src_ref=wown, dst_ref=wseq.at[d - 1], send_sem=wss.at[d - 1], recv_sem=wsr.at[d - 1],
            device_id={"seq": (me + d) % n_seq}, device_id_type=MESH,
        )

    def w_dp(d):
        return pltpu.make_async_remote_copy(
            src_ref=wrow, dst_ref=wdp.at[d - 1], send_sem=wds.at[d - 1], recv_sem=wdr.at[d - 1],
            device_id={"dp": (row + d) % n_dp}, device_id_type=MESH,
        )

    pl.semaphore_wait(barrier, n_seq + n_dp - 2)

    def start_w(d, _):
        w_seq(d).start()
        return 0

    def fresh_step(c, _):
        e = spread(c)
        run_x = mm(run_hi, e) + mm(run_lo, e)
        rise = jnp.exp(run_x)
        inv = jnp.exp(-run_x)
        lifted = (f_ref[:, lanes(c)].astype(F32) * inv).astype(BF16)
        gain = rise[length - 1:length]
        xf_send[c, 0:state, :] = mm(keys_t, lifted) * (gain * sigma)
        xf_send[c, state:state + EXTRA, :] = jnp.broadcast_to(gain * whole_block, (EXTRA, CHUNK))
        to_partner(xf_send, xf_recv, xfs, xfr, c).start()
        rise_s[c] = rise
        inv_s[c] = inv
        lift_s[c] = lifted
        return 0

    lax.fori_loop(0, chunks, fresh_step, 0)
    lax.fori_loop(1, n_seq, start_w, 0)

    linked = (rows_i >= cols_i) & (seg_col == seg_row)
    linked_t = (rows_i <= cols_i) & (seg_col == seg_row)
    mixing = jnp.where(linked, mm_nt(queries, keys) * sigma, 0.0).astype(BF16)
    mixing_t = jnp.where(linked_t, mm_nt(keys, queries) * sigma, 0.0).astype(BF16)

    @pl.when(pair == 0)
    def _():
        zf_recv[...] = jnp.zeros_like(zf_recv)

    @pl.when(pair == pairs - 1)
    def _():
        zb_recv[...] = jnp.zeros_like(zb_recv)

    dmix_s[...] = jnp.zeros_like(dmix_s)
    dmixt_s[...] = jnp.zeros_like(dmixt_s)
    dq_s[...] = jnp.zeros_like(dq_s)
    dk_s[...] = jnp.zeros_like(dk_s)
    rt_s[...] = jnp.zeros_like(rt_s)
    ex_s[...] = jnp.zeros_like(ex_s)

    def inner_step(c, _):
        y_s[c] = mm(mixing, lift_s[c])
        return 0

    def add_w(d, total):
        w_seq(d).wait_recv()
        return total + wseq[d - 1]

    wrow[...] = lax.fori_loop(1, n_seq, add_w, wown[...])

    def start_d(d, _):
        w_dp(d).start()
        return 0

    lax.fori_loop(1, n_dp, start_d, 0)
    lax.fori_loop(0, chunks, inner_step, 0)

    def add_d(d, total):
        w_dp(d).wait_recv()
        return total + wdp[d - 1]

    total = lax.fori_loop(1, n_dp, add_d, wrow[...])
    mean_weight = total[0:1, 0:1] * (1.0 / (length * n_seq * n_dp))
    weight = turned[:, heads + 8:heads + 9] / mean_weight

    def forward_step(c, _):
        to_partner(xf_send, xf_recv, xfs, xfr, c).wait_recv()

        @pl.when(pair > 0)
        def _():
            to_pair(zf_send, zf_recv, zfs, zfr, c, me).wait_recv()

        own = xf_send[c, 0:state, :]
        own_keep = xf_send[c, state:state + 1, :]
        other = xf_recv[c, 0:state, :]
        other_keep = xf_recv[c, state:state + 1, :]
        entry = zf_recv[c]
        before = jnp.where(odd, other + other_keep * entry, entry)
        after = own + own_keep * before
        zf_send[c] = jnp.where(odd, after, other + other_keep * after)

        @pl.when(pair < pairs - 1)
        def _():
            to_pair(zf_send, zf_recv, zfs, zfr, c, me + 2).start()

        so_s[c] = after
        before_h = before.astype(BF16)
        rise = rise_s[c]
        y = rise * (y_s[c] + mm(queries_open, before_h))
        out_ref[:, lanes(c)] = y.astype(BF16)
        grad = weight * (y - t_ref[:, lanes(c)].astype(F32))
        z = (grad * rise).astype(BF16)
        xb_send[c] = mm(queries_t, z)
        to_partner(xb_send, xb_recv, xbs, xbr, c).start()
        y_s[c] = grad * y
        dq_s[...] += mm_nt(z, before_h)
        lifted = lift_s[c]
        dmix_s[...] += mm_nt(z, lifted)
        dmixt_s[...] += mm_nt(lifted, z)
        dl_s[c] = mm(mixing_t, z)
        return 0

    lax.fori_loop(0, chunks, forward_step, 0)

    def backward_step(c, _):
        to_partner(xb_send, xb_recv, xbs, xbr, c).wait_recv()

        @pl.when(pair < pairs - 1)
        def _():
            to_pair(zb_send, zb_recv, zbs, zbr, c, me).wait_recv()

        own = xb_send[c]
        own_keep = xf_send[c, state:state + 1, :]
        other = xb_recv[c]
        other_keep = xf_recv[c, state:state + 1, :]
        entry = zb_recv[c]
        adjoint = jnp.where(odd, entry, other + other_keep * entry)
        onward = own + own_keep * adjoint
        zb_send[c] = jnp.where(odd, other + other_keep * onward, onward)

        @pl.when(pair > 0)
        def _():
            to_pair(zb_send, zb_recv, zbs, zbr, c, me - 2).start()

        e = spread(c)
        gain = rise_s[c, length - 1:length, :]
        scaled = (adjoint * (gain * sigma)).astype(BF16)
        d_feature = inv_s[c] * (dl_s[c] + mm(keys_tail, scaled))
        gf_ref[:, lanes(c)] = d_feature.astype(BF16)
        change = y_s[c] - f_ref[:, lanes(c)].astype(F32) * d_feature
        change_hi, change_lo = split(change)
        rt_s[...] += mm_nt(e, change_hi) + mm_nt(e, change_lo)
        dk_s[...] += mm_nt(lift_s[c], scaled)
        end_hi, end_lo = split(adjoint * so_s[c])
        ex_s[...] += mm_nt(e, end_hi) + mm_nt(e, end_lo)
        return 0

    lax.fori_loop(0, chunks, backward_step, 0)

    d_scores = (jnp.where(linked, dmix_s[...], 0.0) * sigma).astype(BF16)
    d_scores_t = (jnp.where(linked_t, dmixt_s[...], 0.0) * sigma).astype(BF16)
    gq_ref[...] = (mm(d_scores, keys) + open_col * dq_s[...]).astype(BF16)
    gk_ref[...] = (mm(d_scores_t, queries) + tail_col * dk_s[...]).astype(BF16)
    rt_hi, rt_lo = split(rt_s[...])
    decay = mm(rt_hi, lower) + mm(rt_lo, lower) + jnp.sum(ex_s[...], axis=1, keepdims=True)
    gd_ref[...] = decay[:heads]

    def finish_step(c, _):
        to_partner(xf_send, xf_recv, xfs, xfr, c).wait_send()
        to_partner(xb_send, xb_recv, xbs, xbr, c).wait_send()

        @pl.when(pair < pairs - 1)
        def _():
            to_pair(zf_send, zf_recv, zfs, zfr, c, me + 2).wait_send()

        @pl.when(pair > 0)
        def _():
            to_pair(zb_send, zb_recv, zbs, zbr, c, me - 2).wait_send()

        return 0

    lax.fori_loop(0, chunks, finish_step, 0)

    def finish_w(d, _):
        w_seq(d).wait_send()
        return 0

    def finish_d(d, _):
        w_dp(d).wait_send()
        return 0

    lax.fori_loop(1, n_seq, finish_w, 0)
    lax.fori_loop(1, n_dp, finish_d, 0)


def body(features, key_proj, query_proj, log_decay, doc_start, loss_weight, target):
    n_seq, n_dp = lax.axis_size("seq"), lax.axis_size("dp")
    length, width = features.shape[1:]
    state = key_proj.shape[2]
    heads = log_decay.shape[1]
    chunks = width // CHUNK
    vmem = pl.BlockSpec(memory_space=pltpu.VMEM)
    big = (chunks, length, CHUNK)
    small = (chunks, state, CHUNK)
    padded = (chunks, state + EXTRA, CHUNK)
    scratch = [
        pltpu.VMEM(padded, F32), pltpu.VMEM(padded, F32),
        pltpu.VMEM(small, F32), pltpu.VMEM(small, F32),
        pltpu.VMEM(small, F32), pltpu.VMEM(small, F32),
        pltpu.VMEM(small, F32), pltpu.VMEM(small, F32),
        pltpu.VMEM(big, F32), pltpu.VMEM(big, F32), pltpu.VMEM(big, F32), pltpu.VMEM(big, F32),
        pltpu.VMEM(big, BF16), pltpu.VMEM(small, F32),
        pltpu.VMEM((length, length), F32), pltpu.VMEM((length, length), F32),
        pltpu.VMEM((length, state), F32), pltpu.VMEM((length, state), F32),
        pltpu.VMEM((128, length), F32), pltpu.VMEM((128, state), F32),
        pltpu.VMEM((8, 128), F32), pltpu.VMEM((n_seq - 1, 8, 128), F32),
        pltpu.VMEM((8, 128), F32), pltpu.VMEM((n_dp - 1, 8, 128), F32),
    ]
    scratch += [pltpu.SemaphoreType.DMA((chunks,))] * 8
    scratch += [pltpu.SemaphoreType.DMA((n_seq - 1,))] * 2
    scratch += [pltpu.SemaphoreType.DMA((n_dp - 1,))] * 2
    results = pl.pallas_call(
        functools.partial(kernel, n_seq, n_dp, heads),
        out_shape=(
            jax.ShapeDtypeStruct((length, width), BF16),
            jax.ShapeDtypeStruct((length, width), BF16),
            jax.ShapeDtypeStruct((length, state), BF16),
            jax.ShapeDtypeStruct((length, state), BF16),
            jax.ShapeDtypeStruct((heads, length), F32),
        ),
        in_specs=[vmem] * 7,
        out_specs=(vmem,) * 5,
        scratch_shapes=scratch,
        compiler_params=pltpu.CompilerParams(
            collective_id=0, has_side_effects=True, vmem_limit_bytes=48 << 20
        ),
        name="mixing",
    )(
        features[0], key_proj[0], query_proj[0], log_decay[0], doc_start, loss_weight, target[0]
    )
    return tuple(r[None] for r in results)


def solution(mesh):
    placed = (
        P("dp", "seq", None),
        P("dp", "seq", None),
        P("dp", "seq", None),
        P("dp", None, "seq"),
        P("dp", "seq"),
        P("dp", "seq"),
        P("dp", "seq", None),
    )
    return jax.shard_map(
        body,
        mesh=mesh,
        in_specs=placed,
        out_specs=(
            P("dp", "seq", None),
            P("dp", "seq", None),
            P("dp", "seq", None),
            P("dp", "seq", None),
            P("dp", None, "seq"),
        ),
        check_vma=False,
    )
```

time: 242 us -> 113 us (0.47)
  Pallas kernels: 0 us -> 102 us
  waiting for transfers between devices: 90.5 us -> 0 us
  blocking collectives: 41.3 us -> 0 us
  matrix products: 33.3 us -> 0 us
  starting transfers between devices: 32.7 us -> 0 us
  other arithmetic: 16.6 us -> 0 us
  local copies, waits for them, and re-layouts: 23.4 us -> 9.38 us
    pallas_call x0 -> x1, Pallas kernels: none -> 102 us  [body(): pl.pallas_call(functools.partial(kernel, n_seq, n_dp, heads), out_shape=(...]
    ppermute x10 -> x0, waiting for transfers between devices: 90.5 us -> none  [from_behind(): return lax.ppermute(block, axis, route)]
    psum x1 -> x0, blocking collectives: 41.3 us -> none  [body(): weight_sum = lax.psum(jnp.sum(weight), ('seq', 'dp'))]
    dot_general x12 -> x0, matrix products: 33.3 us -> none  [the longest x3 11.9 us: block_tail(): jnp.einsum('sn,shp->hpn', key_rows, values * tail_weight.T[:, :, None], p...]
    ppermute x10 -> x0, starting transfers between devices: 32.7 us -> none  [from_behind(): return lax.ppermute(block, axis, route)]
    convert_element_type x2 -> x0, local copies, waits for them, and re-layouts: 5.17 us -> none  [the longest x1 2.63 us: block_step(): (values * jnp.exp(-running).T[:, :, None]).astype(jnp.bfloat16)]
    reduce_sum x4 -> x0, local copies, waits for them, and re-layouts: 4.75 us -> none  [the longest x1 1.51 us: block_step(): jnp.einsum('tn,hpn->thp', query_rows, carry_state, precision=exact_mode)]
    another operation x8 -> x0, other arithmetic: 4.38 us -> none
  transfers between devices with their start and end apart: 10 -> 0, of which waited for: 6 -> 0; matrix products, arithmetic and copies ran while one was open for 14% -> 0% of each run, Pallas kernels for 0% -> 0%
where the time goes in v1:
time: 113 us; the launch traced here: 112 us
  Pallas kernels  102 us (90%)
  local copies, waits for them, and re-layouts  9.38 us (8%)
    pallas_call x1, Pallas kernels, body(): pl.pallas_call(functools.partial(kernel, n_seq, n_dp, heads), out_shape=(...  102 us
    unnamed x19, local copies, waits for them, and re-layouts  9.38 us

profile of v1, /device:TPU:0, one launch (start us, length us, event | category | flops | bytes accessed | tf_op | source)
XLA Modules:
  0.0 112.3 jit_solution(141312084628437583)
XLA Ops:
  0.6 0.0 copy-start.6
  0.6 0.0 copy-start.5
  0.7 0.7 copy-done.6
  1.3 0.0 copy-done.5
  1.3 0.0 copy-start
  1.3 1.2 %copy-done = bf16[1,256,2048]{2,1,0:T(8,128)(2,1)S(1)} copy-done((bf16[1,256,2048]{2,1,0:T(8,128)(2,1)S(1)}, bf16[1,256,2048]{2,1,0:T(8,128)(2,1)}, u32[]{:S(2)}) %copy-start) | copy-done | bytes 1048600
  2.6 0.0 copy-start.1
  2.6 1.2 %copy-done.1 = bf16[1,256,2048]{2,1,0:T(8,128)(2,1)S(1)} copy-done((bf16[1,256,2048]{2,1,0:T(8,128)(2,1)S(1)}, bf16[1,256,2048]{2,1,0:T(8,128)(2,1)}, u32[]{:S(2)}) %copy-start.1) | copy-done | bytes 1048600
  3.8 0.0 copy-start.2
  3.8 0.8 copy-done.2
  4.6 0.0 copy-start.3
  4.6 0.8 copy-done.3
  5.5 0.0 copy-start.4
  5.5 0.8 copy-done.4
  6.2 102.2 %mixing.1 = (bf16[256,2048]{1,0:T(8,128)(2,1)S(1)}, bf16[256,2048]{1,0:T(8,128)(2,1)S(1)}, bf16[256,128]{1,0:T(8,128)(2,1)S(1)}, bf16[256,128]{1,0:T(8,128)(2,1)S(1)}, f32[32,256]{1,0:T(8,128)S(1)}) custom-call(bf16[256,2048]{1,0:T(8,128)(2,1)S(1)} %bitcast.10, bf16[256,128]{1,0:T(8,128)(2,1)S(1)} %bitcast.14, bf16[256,128]{1,0:T(8,128)(2,1)S(1)} %bitcast.15, ...), custom_call_target="tpu_custom_call" | custom-call | tf_op jit(solution)/shard_map/mixing/pallas_call | solution.py:350
  108.5 1.0 copy.17
  109.4 1.0 copy.18
  110.4 0.6 copy.19
  111.0 0.6 copy.20
  111.7 0.6 copy.21
Async XLA Ops:
  0.6 0.7 copy-start.6
  0.6 0.7 copy-start.5
  1.3 1.2 %copy-start = (bf16[1,256,2048]{2,1,0:T(8,128)(2,1)S(1)}, bf16[1,256,2048]{2,1,0:T(8,128)(2,1)}, u32[]{:S(2)}) copy-start(bf16[1,256,2048]{2,1,0:T(8,128)(2,1)} %param.7) | copy-start | bytes 3145732
  2.6 1.2 %copy-start.1 = (bf16[1,256,2048]{2,1,0:T(8,128)(2,1)S(1)}, bf16[1,256,2048]{2,1,0:T(8,128)(2,1)}, u32[]{:S(2)}) copy-start(bf16[1,256,2048]{2,1,0:T(8,128)(2,1)} %param.13) | copy-start | bytes 3145732
  3.8 0.8 copy-start.2
  4.6 0.8 copy-start.3
  5.5 0.8 copy-start.4

commit v2 on v1

--- a/solution.py
+++ b/solution.py
@@ -11,8 +11,10 @@
 F32 = jnp.float32
 BF16 = jnp.bfloat16
 MESH = pl.DeviceIdType.MESH
-CHUNK = 256
+CHUNK = 128
 EXTRA = 8
+LAG_LAST = 2
+LAG_PAIR = 5
 
 
 def mm(a, b):
@@ -31,12 +33,13 @@
 
 def kernel(
     n_seq, n_dp, heads,
-    f_ref, k_ref, q_ref, ld_ref, ds_ref, w_ref, t_ref,
+    f_hbm, k_hbm, q_hbm, ld_hbm, ds_hbm, w_hbm, t_hbm,
     out_ref, gf_ref, gk_ref, gq_ref, gd_ref,
     xf_send, xf_recv, zf_send, zf_recv, xb_send, xb_recv, zb_send, zb_recv,
     rise_s, inv_s, y_s, dl_s, lift_s, so_s,
-    dmix_s, dmixt_s, dq_s, dk_s, rt_s, ex_s,
+    dmix_s, dmixt_s, dq_s, dk_s, gk_s, rt_s, ex_s,
     wown, wseq, wrow, wdp,
+    f_ref, k_ref, q_ref, ld_ref, ds_ref, w_ref, t_ref, in_sem,
     xfs, xfr, zfs, zfr, xbs, xbr, zbs, zbr, wss, wsr, wds, wdr,
 ):
     length, width = f_ref.shape
@@ -54,6 +57,17 @@
     odd = is_odd == 1
     partner = me + 1 - 2 * is_odd
 
+    fetches = [
+        pltpu.make_async_copy(src, dst, in_sem.at[i])
+        for i, (src, dst) in enumerate(
+            [
+                (ld_hbm, ld_ref), (ds_hbm, ds_ref), (w_hbm, w_ref), (k_hbm, k_ref),
+                (q_hbm, q_ref), (f_hbm, f_ref), (t_hbm, t_ref),
+            ]
+        )
+    ]
+    for fetch in fetches:
+        fetch.start()
     barrier = pltpu.get_barrier_semaphore()
 
     def greet_seq(d, _):
@@ -71,6 +85,8 @@
     lax.fori_loop(1, n_seq, greet_seq, 0)
     lax.fori_loop(1, n_dp, greet_dp, 0)
 
+    for fetch in fetches[:5]:
+        fetch.wait()
     wown[...] = jnp.broadcast_to(jnp.sum(w_ref[...], axis=1, keepdims=True), wown.shape)
 
     starts = ds_ref[...].astype(F32)
@@ -163,8 +179,23 @@
         lift_s[c] = lifted
         return 0
 
-    lax.fori_loop(0, chunks, fresh_step, 0)
     lax.fori_loop(1, n_seq, start_w, 0)
+    fetches[5].wait()
+    first = chunks // 4
+    lax.fori_loop(0, first, fresh_step, 0)
+
+    def add_w(d, total):
+        w_seq(d).wait_recv()
+        return total + wseq[d - 1]
+
+    wrow[...] = lax.fori_loop(1, n_seq, add_w, wown[...])
+
+    def start_d(d, _):
+        w_dp(d).start()
+        return 0
+
+    lax.fori_loop(1, n_dp, start_d, 0)
+    lax.fori_loop(first, chunks, fresh_step, 0)
 
     linked = (rows_i >= cols_i) & (seg_col == seg_row)
     linked_t = (rows_i <= cols_i) & (seg_col == seg_row)
@@ -190,17 +221,6 @@
         y_s[c] = mm(mixing, lift_s[c])
         return 0
 
-    def add_w(d, total):
-        w_seq(d).wait_recv()
-        return total + wseq[d - 1]
-
-    wrow[...] = lax.fori_loop(1, n_seq, add_w, wown[...])
-
-    def start_d(d, _):
-        w_dp(d).start()
-        return 0
-
-    lax.fori_loop(1, n_dp, start_d, 0)
     lax.fori_loop(0, chunks, inner_step, 0)
 
     def add_d(d, total):
@@ -208,8 +228,10 @@
         return total + wdp[d - 1]
 
     total = lax.fori_loop(1, n_dp, add_d, wrow[...])
-    mean_weight = total[0:1, 0:1] * (1.0 / (length * n_seq * n_dp))
-    weight = turned[:, heads + 8:heads + 9] / mean_weight
+    over_mean = (length * n_seq * n_dp) / total[0:1, 0:1]
+
+    fetches[6].wait()
+    weight = turned[:, heads + 8:heads + 9]
 
     def forward_step(c, _):
         to_partner(xf_send, xf_recv, xfs, xfr, c).wait_recv()
@@ -248,8 +270,6 @@
         dl_s[c] = mm(mixing_t, z)
         return 0
 
-    lax.fori_loop(0, chunks, forward_step, 0)
-
     def backward_step(c, _):
         to_partner(xb_send, xb_recv, xbs, xbr, c).wait_recv()
 
@@ -272,10 +292,11 @@
 
         e = spread(c)
         gain = rise_s[c, length - 1:length, :]
+        adjoint = adjoint * over_mean
         scaled = (adjoint * (gain * sigma)).astype(BF16)
-        d_feature = inv_s[c] * (dl_s[c] + mm(keys_tail, scaled))
+        d_feature = inv_s[c] * (dl_s[c] * over_mean + mm(keys_tail, scaled))
         gf_ref[:, lanes(c)] = d_feature.astype(BF16)
-        change = y_s[c] - f_ref[:, lanes(c)].astype(F32) * d_feature
+        change = y_s[c] * over_mean - f_ref[:, lanes(c)].astype(F32) * d_feature
         change_hi, change_lo = split(change)
         rt_s[...] += mm_nt(e, change_hi) + mm_nt(e, change_lo)
         dk_s[...] += mm_nt(lift_s[c], scaled)
@@ -283,12 +304,32 @@
         ex_s[...] += mm_nt(e, end_hi) + mm_nt(e, end_lo)
         return 0
 
-    lax.fori_loop(0, chunks, backward_step, 0)
-
-    d_scores = (jnp.where(linked, dmix_s[...], 0.0) * sigma).astype(BF16)
-    d_scores_t = (jnp.where(linked_t, dmixt_s[...], 0.0) * sigma).astype(BF16)
-    gq_ref[...] = (mm(d_scores, keys) + open_col * dq_s[...]).astype(BF16)
-    gk_ref[...] = (mm(d_scores_t, queries) + tail_col * dk_s[...]).astype(BF16)
+    def finish_scores():
+        d_scores = (jnp.where(linked, dmix_s[...], 0.0) * (over_mean * sigma)).astype(BF16)
+        d_scores_t = (jnp.where(linked_t, dmixt_s[...], 0.0) * (over_mean * sigma)).astype(BF16)
+        gq_ref[...] = (mm(d_scores, keys) + (open_col * over_mean) * dq_s[...]).astype(BF16)
+        gk_s[...] = mm(d_scores_t, queries)
+
+    lag = jnp.minimum(chunks, LAG_LAST + LAG_PAIR * (pairs - 1 - pair))
+
+    def step(i, _):
+        @pl.when(i < chunks)
+        def _():
+            forward_step(i, 0)
+
+        @pl.when(i == chunks)
+        def _():
+            finish_scores()
+
+        @pl.when((i >= lag) & (i < lag + chunks))
+        def _():
+            backward_step(i - lag, 0)
+
+        return 0
+
+    lax.fori_loop(0, 2 * chunks, step, 0)
+
+    gk_ref[...] = (gk_s[...] + tail_col * dk_s[...]).astype(BF16)
     rt_hi, rt_lo = split(rt_s[...])
     decay = mm(rt_hi, lower) + mm(rt_lo, lower) + jnp.sum(ex_s[...], axis=1, keepdims=True)
     gd_ref[...] = decay[:heads]
@@ -340,9 +381,15 @@
         pltpu.VMEM(big, BF16), pltpu.VMEM(small, F32),
         pltpu.VMEM((length, length), F32), pltpu.VMEM((length, length), F32),
         pltpu.VMEM((length, state), F32), pltpu.VMEM((length, state), F32),
-        pltpu.VMEM((128, length), F32), pltpu.VMEM((128, state), F32),
+        pltpu.VMEM((length, state), F32), pltpu.VMEM((128, length), F32), pltpu.VMEM((128, state), F32),
         pltpu.VMEM((8, 128), F32), pltpu.VMEM((n_seq - 1, 8, 128), F32),
         pltpu.VMEM((8, 128), F32), pltpu.VMEM((n_dp - 1, 8, 128), F32),
+    ]
+    scratch += [
+        pltpu.VMEM((length, width), BF16), pltpu.VMEM((length, state), BF16),
+        pltpu.VMEM((length, state), BF16), pltpu.VMEM((heads, length), F32),
+        pltpu.VMEM((1, length), jnp.int32), pltpu.VMEM((1, length), F32),
+        pltpu.VMEM((length, width), BF16), pltpu.SemaphoreType.DMA((7,)),
     ]
     scratch += [pltpu.SemaphoreType.DMA((chunks,))] * 8
     scratch += [pltpu.SemaphoreType.DMA((n_seq - 1,))] * 2
@@ -356,11 +403,11 @@
             jax.ShapeDtypeStruct((length, state), BF16),
             jax.ShapeDtypeStruct((heads, length), F32),
         ),
-        in_specs=[vmem] * 7,
+        in_specs=[pl.BlockSpec(memory_space=pltpu.HBM)] * 7,
         out_specs=(vmem,) * 5,
         scratch_shapes=scratch,
         compiler_params=pltpu.CompilerParams(
-            collective_id=0, has_side_effects=True, vmem_limit_bytes=48 << 20
+            collective_id=0, has_side_effects=True, vmem_limit_bytes=60 << 20
         ),
         name="mixing",
     )(

time: 113 us -> 75.7 us (0.67)
  Pallas kernels: 102 us -> 69.2 us
  local copies, waits for them, and re-layouts: 9.38 us -> 5.6 us
    pallas_call x1, Pallas kernels: 102 us -> 69.2 us  [body(): pl.pallas_call(functools.partial(kernel, n_seq, n_dp, heads), out_shape=(...]
    unnamed x19 -> x13, local copies, waits for them, and re-layouts: 9.38 us -> 5.6 us
where the time goes in v2:
time: 75.7 us; the launch traced here: 75.4 us
  Pallas kernels  69.2 us (91%)
  local copies, waits for them, and re-layouts  5.6 us (7%)
    pallas_call x1, Pallas kernels, body(): pl.pallas_call(functools.partial(kernel, n_seq, n_dp, heads), out_shape=(...  69.2 us
    unnamed x13, local copies, waits for them, and re-layouts  5.6 us

profile of v2, /device:TPU:0, one launch (start us, length us, event | category | flops | bytes accessed | tf_op | source)
XLA Modules:
  0.0 75.4 jit_solution(4508341386342035802)
XLA Ops:
  0.6 69.2 %mixing.1 = (bf16[256,2048]{1,0:T(8,128)(2,1)}, bf16[256,2048]{1,0:T(8,128)(2,1)}, bf16[256,128]{1,0:T(8,128)(2,1)}, bf16[256,128]{1,0:T(8,128)(2,1)}, f32[32,256]{1,0:T(8,128)}) custom-call(bf16[256,2048]{1,0:T(8,128)(2,1)} %bitcast.10, bf16[256,128]{1,0:T(8,128)(2,1)} %bitcast.14, bf16[256,128]{1,0:T(8,128)(2,1)} %bitcast.15, f32[32,256]{1,0:T(8,128)} %bitcast.18, ...), custom_call_target="tpu_custom_call" | custom-call | tf_op jit(solution)/shard_map/mixing/pallas_call | solution.py:397
  69.8 0.0 copy-start
  69.8 2.4 %copy.17 = bf16[1,256,2048]{2,1,0:T(8,128)(2,1)} copy(bf16[1,256,2048]{2,1,0:T(8,128)(2,1)} %bitcast.13) | data formatting | bytes 2097152
  72.2 0.0 copy-done
  72.2 0.0 copy-start.2
  72.2 1.0 %copy.18 = bf16[1,256,2048]{2,1,0:T(8,128)(2,1)} copy(bf16[1,256,2048]{2,1,0:T(8,128)(2,1)S(1)} %bitcast.12) | data formatting | bytes 2097152
  73.2 0.0 copy-done.2
  73.2 0.0 copy-start.1
  73.2 0.6 copy.19
  73.8 0.2 copy-done.1
  74.0 0.0 copy-start.3
  74.0 0.6 copy.20
  74.7 0.1 copy-done.3
  74.8 0.6 copy.21
Async XLA Ops:
  69.8 2.4 %copy-start = (bf16[256,2048]{1,0:T(8,128)(2,1)S(1)}, bf16[256,2048]{1,0:T(8,128)(2,1)}, u32[]{:S(2)}) copy-start(bf16[256,2048]{1,0:T(8,128)(2,1)} %get-tuple-element.11) | copy-start | bytes 3145732
  72.2 1.0 %copy-start.2 = (bf16[256,128]{1,0:T(8,128)(2,1)S(1)}, bf16[256,128]{1,0:T(8,128)(2,1)}, u32[]{:S(2)}) copy-start(bf16[256,128]{1,0:T(8,128)(2,1)} %get-tuple-element.12) | copy-start | bytes 196612
  73.2 0.9 %copy-start.1 = (bf16[256,128]{1,0:T(8,128)(2,1)S(1)}, bf16[256,128]{1,0:T(8,128)(2,1)}, u32[]{:S(2)}) copy-start(bf16[256,128]{1,0:T(8,128)(2,1)} %get-tuple-element.13) | copy-start | bytes 196612
  74.0 0.8 %copy-start.3 = (f32[32,256]{1,0:T(8,128)S(1)}, f32[32,256]{1,0:T(8,128)}, u32[]{:S(2)}) copy-start(f32[32,256]{1,0:T(8,128)} %get-tuple-element.14) | copy-start | bytes 98308

commit v3 on v2

--- a/solution.py
+++ b/solution.py
@@ -13,7 +13,7 @@
 MESH = pl.DeviceIdType.MESH
 CHUNK = 128
 EXTRA = 8
-LAG_LAST = 2
+LAG_LAST = 3
 LAG_PAIR = 5
 
 

time: 75.7 us -> 74.9 us (0.989)
  Pallas kernels: 69.2 us -> 68.4 us
    pallas_call x1, Pallas kernels: 69.2 us -> 68.4 us  [body(): pl.pallas_call(functools.partial(kernel, n_seq, n_dp, heads), out_shape=(...]
where the time goes in v3:
time: 74.9 us; the launch traced here: 74.6 us
  Pallas kernels  68.4 us (91%)
  local copies, waits for them, and re-layouts  5.6 us (7%)
    pallas_call x1, Pallas kernels, body(): pl.pallas_call(functools.partial(kernel, n_seq, n_dp, heads), out_shape=(...  68.4 us
    unnamed x13, local copies, waits for them, and re-layouts  5.6 us

profile of v3, /device:TPU:0, one launch (start us, length us, event | category | flops | bytes accessed | tf_op | source)
XLA Modules:
  0.0 74.6 jit_solution(15298661814947714154)
XLA Ops:
  0.6 68.4 %mixing.1 = (bf16[256,2048]{1,0:T(8,128)(2,1)}, bf16[256,2048]{1,0:T(8,128)(2,1)}, bf16[256,128]{1,0:T(8,128)(2,1)}, bf16[256,128]{1,0:T(8,128)(2,1)}, f32[32,256]{1,0:T(8,128)}) custom-call(bf16[256,2048]{1,0:T(8,128)(2,1)} %bitcast.10, bf16[256,128]{1,0:T(8,128)(2,1)} %bitcast.14, bf16[256,128]{1,0:T(8,128)(2,1)} %bitcast.15, f32[32,256]{1,0:T(8,128)} %bitcast.18, ...), custom_call_target="tpu_custom_call" | custom-call | tf_op jit(solution)/shard_map/mixing/pallas_call | solution.py:397
  69.0 0.0 copy-start
  69.0 2.4 %copy.17 = bf16[1,256,2048]{2,1,0:T(8,128)(2,1)} copy(bf16[1,256,2048]{2,1,0:T(8,128)(2,1)} %bitcast.13) | data formatting | bytes 2097152
  71.4 0.0 copy-done
  71.4 0.0 copy-start.2
  71.4 1.0 %copy.18 = bf16[1,256,2048]{2,1,0:T(8,128)(2,1)} copy(bf16[1,256,2048]{2,1,0:T(8,128)(2,1)S(1)} %bitcast.12) | data formatting | bytes 2097152
  72.4 0.0 copy-done.2
  72.4 0.0 copy-start.1
  72.4 0.6 copy.19
  73.0 0.2 copy-done.1
  73.3 0.0 copy-start.3
  73.3 0.6 copy.20
  73.9 0.1 copy-done.3
  74.0 0.6 copy.21
Async XLA Ops:
  69.0 2.4 %copy-start = (bf16[256,2048]{1,0:T(8,128)(2,1)S(1)}, bf16[256,2048]{1,0:T(8,128)(2,1)}, u32[]{:S(2)}) copy-start(bf16[256,2048]{1,0:T(8,128)(2,1)} %get-tuple-element.11) | copy-start | bytes 3145732
  71.4 1.0 %copy-start.2 = (bf16[256,128]{1,0:T(8,128)(2,1)S(1)}, bf16[256,128]{1,0:T(8,128)(2,1)}, u32[]{:S(2)}) copy-start(bf16[256,128]{1,0:T(8,128)(2,1)} %get-tuple-element.12) | copy-start | bytes 196612
  72.4 0.9 %copy-start.1 = (bf16[256,128]{1,0:T(8,128)(2,1)S(1)}, bf16[256,128]{1,0:T(8,128)(2,1)}, u32[]{:S(2)}) copy-start(bf16[256,128]{1,0:T(8,128)(2,1)} %get-tuple-element.13) | copy-start | bytes 196612
  73.3 0.8 %copy-start.3 = (f32[32,256]{1,0:T(8,128)S(1)}, f32[32,256]{1,0:T(8,128)}, u32[]{:S(2)}) copy-start(f32[32,256]{1,0:T(8,128)} %get-tuple-element.14) | copy-start | bytes 98308
